TPU v7x, 32 devices: a whole 2x2x4 slice. The times are simulated.
32 devices in a mesh: dp: 8 (over z, x), seq: 4 (over y, core).
Axes of the slice: x: 2, y: 2, z: 4, core: 2. Of those that a mesh axis runs over, the one named last changes fastest.
Arguments:
- tokens: bfloat16 [16384, 1024], P(('dp', 'seq')), may hold values from -6 to 6
- time_embed: bfloat16 [32, 1024], P(('dp', 'seq')), may hold values from -6 to 6
- lengths: int32 [32], P('dp'), may hold values from 0 to 475, as said below
- cotangent: bfloat16 [16384, 1024], P(('dp', 'seq')), may hold values from -6 to 6
- w_query: bfloat16 [1024, 1024], P('seq'), may hold values from -0.1875 to 0.1875
- w_key: bfloat16 [1024, 1024], P('seq'), may hold values from -0.1875 to 0.1875
- w_value: bfloat16 [1024, 1024], P('seq'), may hold values from -0.1875 to 0.1875
- w_out: bfloat16 [1024, 1024], P('seq'), may hold values from -0.75 to 0.75
- w_time: bfloat16 [1024, 1024], P('seq'), may hold values from -0.1875 to 0.1875
- w_in: bfloat16 [4096, 1024], P('seq'), may hold values from -0.1875 to 0.1875
- w_down: bfloat16 [4096, 1024], P('seq'), may hold values from -0.09375 to 0.09375
- b_query: bfloat16 [1024], replicated, may hold values from -3 to 3
- b_value: bfloat16 [1024], replicated, may hold values from -3 to 3
- b_out: bfloat16 [1024], replicated, may hold values from -3 to 3
- b_time: bfloat16 [1024], replicated, may hold values from -3 to 3
- b_in: bfloat16 [4096], replicated, may hold values from -3 to 3
- b_down: bfloat16 [1024], replicated, may hold values from -2 to 2
- gain_one: bfloat16 [1024], replicated, may hold values from 0.25 to 1.75
- shift_one: bfloat16 [1024], replicated, may hold values from -2 to 2
- gain_two: bfloat16 [1024], replicated, may hold values from 0.25 to 1.75
- shift_two: bfloat16 [1024], replicated, may hold values from -2 to 2
Outputs:
- layer_out: bfloat16 [16384, 1024], P(('dp', 'seq'))
- grad_tokens: bfloat16 [16384, 1024], P(('dp', 'seq'))
- grad_w_query: float32 [1024, 1024], P('seq')
- grad_w_key: float32 [1024, 1024], P('seq')
- grad_w_value: float32 [1024, 1024], P('seq')
- grad_w_out: float32 [1024, 1024], P('seq')
- grad_w_time: float32 [1024, 1024], P('seq')
- grad_w_in: float32 [4096, 1024], P('seq')
- grad_w_down: float32 [4096, 1024], P('seq')
- grad_b_query: float32 [1024], replicated
- grad_b_value: float32 [1024], replicated
- grad_b_out: float32 [1024], replicated
- grad_b_time: float32 [1024], replicated
- grad_b_in: float32 [4096], replicated
- grad_b_down: float32 [1024], replicated
- grad_gain_one: float32 [1024], replicated
- grad_shift_one: float32 [1024], replicated
- grad_gain_two: float32 [1024], replicated
- grad_shift_two: float32 [1024], replicated
Inputs may be any that keep to these rules, and one draw needn't show every extreme that they name: Item i's valid slots are its first lengths[i] + 25; every draw has an item of length 475 and one of length 0.
All inputs are finite; a program needn't handle non-finite values.
Results may differ from a plain program's by a relative error of at most 0.02.
Values may be sent and summed in bfloat16 or wider, within the bound.
A program may use at most 256 MiB of HBM per device.

v0:
```python
import jax
import jax.numpy as jnp
from jax import lax
from jax.sharding import PartitionSpec as P

HEAD_DIM = 64
BLOCK = 25
norm_eps = 1e-05
neg_large = -1e30


def layer_norm(values, gain, shift):
    center = values - jnp.mean(values, axis=-1, keepdims=True)
    spread = lax.rsqrt(jnp.mean(center * center, axis=-1, keepdims=True) + norm_eps)
    return center * spread * gain + shift


def exact_gelu(values):
    return jax.nn.gelu(values, approximate=False)


def split_heads(rows):
    return rows.reshape(rows.shape[0], rows.shape[1] // HEAD_DIM, HEAD_DIM)


def item_scores(item_block, key_valid):
    queries = split_heads(item_block[:, 0])
    key_heads = split_heads(item_block[:, 1])
    value_heads = split_heads(item_block[:, 2])
    scores = jnp.einsum(
        "qhd,khd->hqk", queries, key_heads, preferred_element_type=jnp.float32
    ) * HEAD_DIM ** (-0.5)
    masked = jnp.where(key_valid[None, None, :], scores, neg_large)
    return (queries, key_heads, value_heads, masked)


def attend_forward(packed):
    item_block, key_valid = packed
    queries, key_heads, value_heads, masked = item_scores(item_block, key_valid)
    row_max = jnp.max(masked, axis=-1, keepdims=True)
    exp_scores = jnp.exp(masked - row_max)
    row_total = jnp.sum(exp_scores, axis=-1, keepdims=True)
    soft_weights = (exp_scores / row_total).astype(jnp.bfloat16)
    mixed_heads = jnp.einsum(
        "hqk,khd->qhd", soft_weights, value_heads, preferred_element_type=jnp.float32
    )
    log_total = row_max[:, :, 0] + jnp.log(row_total[:, :, 0])
    return (mixed_heads.reshape(item_block.shape[0], -1).astype(jnp.bfloat16), log_total)


def attend_backward(packed):
    item_block, key_valid, log_total, grad_block = packed
    queries, key_heads, value_heads, masked = item_scores(item_block, key_valid)
    soft_weights = jnp.exp(masked - log_total[:, :, None])
    grad_heads = split_heads(grad_block)
    grad_value = jnp.einsum(
        "hqk,qhd->khd",
        soft_weights.astype(jnp.bfloat16),
        grad_heads,
        preferred_element_type=jnp.float32,
    )
    grad_soft = jnp.einsum(
        "qhd,khd->hqk", grad_heads, value_heads, preferred_element_type=jnp.float32
    )
    grad_scores = soft_weights * (
        grad_soft - jnp.sum(soft_weights * grad_soft, axis=-1, keepdims=True)
    )
    scores_low = grad_scores.astype(jnp.bfloat16)
    score_scale = HEAD_DIM ** (-0.5)
    grad_query = (
        jnp.einsum("hqk,khd->qhd", scores_low, key_heads, preferred_element_type=jnp.float32)
        * score_scale
    )
    grad_key = (
        jnp.einsum("hqk,qhd->khd", scores_low, queries, preferred_element_type=jnp.float32)
        * score_scale
    )
    slot_count = item_block.shape[0]
    return jnp.stack(
        [
            grad_query.reshape(slot_count, -1),
            grad_key.reshape(slot_count, -1),
            grad_value.reshape(slot_count, -1),
        ],
        axis=1,
    ).astype(jnp.bfloat16)


def local(
    tokens,
    time_embed,
    lengths,
    cotangent,
    w_query,
    w_key,
    w_value,
    w_out,
    w_time,
    w_in,
    w_down,
    b_query,
    b_value,
    b_out,
    b_time,
    b_in,
    b_down,
    gain_one,
    shift_one,
    gain_two,
    shift_two,
):
    seq_rank = lax.axis_index("seq")
    item_count = time_embed.shape[0]
    token_count = tokens.shape[0]
    slot_count = token_count // item_count
    model_width = tokens.shape[1]
    full_query, full_key, full_value, full_out, full_time, full_in, full_down = (
        lax.all_gather(w_query, "seq", axis=0, tiled=True),
        lax.all_gather(w_key, "seq", axis=0, tiled=True),
        lax.all_gather(w_value, "seq", axis=0, tiled=True),
        lax.all_gather(w_out, "seq", axis=0, tiled=True),
        lax.all_gather(w_time, "seq", axis=0, tiled=True),
        lax.all_gather(w_in, "seq", axis=0, tiled=True),
        lax.all_gather(w_down, "seq", axis=0, tiled=True),
    )
    bias_query = b_query.astype(jnp.float32)
    bias_value = b_value.astype(jnp.float32)
    bias_out = b_out.astype(jnp.float32)
    bias_time = b_time.astype(jnp.float32)
    bias_in = b_in.astype(jnp.float32)
    bias_down = b_down.astype(jnp.float32)
    gain_first = gain_one.astype(jnp.float32)
    shift_first = shift_one.astype(jnp.float32)
    gain_last = gain_two.astype(jnp.float32)
    shift_last = shift_two.astype(jnp.float32)
    slot_index = lax.broadcasted_iota(jnp.int32, (lengths.shape[0], slot_count), 1)
    group_valid = slot_index < lengths[:, None] + BLOCK
    own_valid = lax.dynamic_slice_in_dim(group_valid, seq_rank * item_count, item_count, 0)
    row_keep = own_valid.reshape(token_count, 1).astype(jnp.float32)
    time_proj = jnp.dot(time_embed, full_time, preferred_element_type=jnp.float32) + bias_time
    resid = (tokens.reshape(item_count, slot_count, model_width) + time_proj[:, None, :]).reshape(
        token_count, model_width
    )
    resid_low = resid.astype(jnp.bfloat16)
    query_rows = (
        jnp.dot(resid_low, full_query, preferred_element_type=jnp.float32) + bias_query
    ).astype(jnp.bfloat16)
    key_rows = jnp.dot(resid_low, full_key, preferred_element_type=jnp.float32).astype(jnp.bfloat16)
    value_rows = (
        jnp.dot(resid_low, full_value, preferred_element_type=jnp.float32) + bias_value
    ).astype(jnp.bfloat16)
    stacked = jnp.stack([query_rows, key_rows, value_rows], axis=1).reshape(
        item_count, slot_count, 3, model_width
    )
    head_side = lax.all_to_all(stacked, "seq", split_axis=3, concat_axis=0, tiled=True)
    mixed_heads, log_totals = lax.map(attend_forward, (head_side, group_valid))
    mixed_rows = lax.all_to_all(
        mixed_heads, "seq", split_axis=0, concat_axis=2, tiled=True
    ).reshape(token_count, model_width)
    attn_out = jnp.dot(mixed_rows, full_out, preferred_element_type=jnp.float32) + bias_out
    first_norm, first_pull = jax.vjp(layer_norm, resid + attn_out, gain_first, shift_first)
    first_low = first_norm.astype(jnp.bfloat16)
    hidden_pre = (
        jnp.einsum("td,fd->tf", first_low, full_in, preferred_element_type=jnp.float32) + bias_in
    )
    hidden, gelu_pull = jax.vjp(exact_gelu, hidden_pre)
    hidden_low = hidden.astype(jnp.bfloat16)
    ffn_out = jnp.dot(hidden_low, full_down, preferred_element_type=jnp.float32) + bias_down
    second_norm, second_pull = jax.vjp(layer_norm, first_norm + ffn_out, gain_last, shift_last)
    layer_out = (second_norm * row_keep).astype(jnp.bfloat16)
    back_query, back_key, back_value, back_out, back_in, back_down = (
        lax.all_gather(w_query, "seq", axis=0, tiled=True),
        lax.all_gather(w_key, "seq", axis=0, tiled=True),
        lax.all_gather(w_value, "seq", axis=0, tiled=True),
        lax.all_gather(w_out, "seq", axis=0, tiled=True),
        lax.all_gather(w_in, "seq", axis=0, tiled=True),
        lax.all_gather(w_down, "seq", axis=0, tiled=True),
    )
    grad_second_in, grad_gain_two, grad_shift_two = second_pull(
        cotangent.astype(jnp.float32) * row_keep
    )
    grad_ffn = grad_second_in.astype(jnp.bfloat16)
    grad_hidden = jnp.einsum("td,fd->tf", grad_ffn, back_down, preferred_element_type=jnp.float32)
    grad_pre = gelu_pull(grad_hidden)[0].astype(jnp.bfloat16)
    grad_first = grad_second_in + jnp.dot(grad_pre, back_in, preferred_element_type=jnp.float32)
    grad_first_in, grad_gain_one, grad_shift_one = first_pull(grad_first)
    grad_attn = grad_first_in.astype(jnp.bfloat16)
    grad_mixed = jnp.einsum(
        "td,ed->te", grad_attn, back_out, preferred_element_type=jnp.float32
    ).astype(jnp.bfloat16)
    grad_heads = lax.all_to_all(
        grad_mixed.reshape(item_count, slot_count, model_width),
        "seq",
        split_axis=2,
        concat_axis=0,
        tiled=True,
    )
    grad_stack = lax.map(attend_backward, (head_side, group_valid, log_totals, grad_heads))
    grad_qkv = lax.all_to_all(grad_stack, "seq", split_axis=0, concat_axis=3, tiled=True).reshape(
        token_count, 3, model_width
    )
    grad_query_rows = grad_qkv[:, 0]
    grad_key_rows = grad_qkv[:, 1]
    grad_value_rows = grad_qkv[:, 2]
    grad_resid = grad_first_in + jnp.einsum(
        "te,de->td", grad_query_rows, back_query, preferred_element_type=jnp.float32
    )
    grad_resid = grad_resid + jnp.einsum(
        "te,de->td", grad_key_rows, back_key, preferred_element_type=jnp.float32
    )
    grad_resid = grad_resid + jnp.einsum(
        "te,de->td", grad_value_rows, back_value, preferred_element_type=jnp.float32
    )
    grad_tokens = grad_resid.astype(jnp.bfloat16)
    grad_time = jnp.sum(grad_resid.reshape(item_count, slot_count, model_width), axis=1).astype(
        jnp.bfloat16
    )
    term_in = jnp.einsum("tf,td->fd", grad_pre, first_low, preferred_element_type=jnp.float32)
    term_down = jnp.einsum("tf,td->fd", hidden_low, grad_ffn, preferred_element_type=jnp.float32)
    ffn_share = lax.psum_scatter(
        jnp.concatenate([term_in, term_down], axis=1).astype(jnp.bfloat16),
        "seq",
        scatter_dimension=0,
        tiled=True,
    ).astype(jnp.float32)
    share_in = ffn_share[:, :model_width]
    share_down = ffn_share[:, model_width:]
    grad_qkv_flat = grad_qkv.reshape(token_count, 3 * model_width)
    term_qkv = jnp.einsum("tr,te->re", resid_low, grad_qkv_flat, preferred_element_type=jnp.float32)
    term_out = jnp.einsum("tr,te->re", mixed_rows, grad_attn, preferred_element_type=jnp.float32)
    term_time = jnp.einsum("tr,te->re", time_embed, grad_time, preferred_element_type=jnp.float32)
    attn_share = lax.psum_scatter(
        jnp.concatenate([term_qkv, term_out, term_time], axis=1).astype(jnp.bfloat16),
        "seq",
        scatter_dimension=0,
        tiled=True,
    ).astype(jnp.float32)
    sum_in, sum_down, sum_attn = lax.psum((share_in, share_down, attn_share), "dp")
    (
        grad_b_query,
        grad_b_value,
        grad_b_out,
        grad_b_time,
        grad_b_in,
        grad_b_down,
        sum_gain_one,
        sum_shift_one,
        sum_gain_two,
        sum_shift_two,
    ) = lax.psum(
        (
            jnp.sum(grad_query_rows, axis=0, dtype=jnp.float32),
            jnp.sum(grad_value_rows, axis=0, dtype=jnp.float32),
            jnp.sum(grad_attn, axis=0, dtype=jnp.float32),
            jnp.sum(grad_time, axis=0, dtype=jnp.float32),
            jnp.sum(grad_pre, axis=0, dtype=jnp.float32),
            jnp.sum(grad_ffn, axis=0, dtype=jnp.float32),
            grad_gain_one,
            grad_shift_one,
            grad_gain_two,
            grad_shift_two,
        ),
        ("dp", "seq"),
    )
    return (
        layer_out,
        grad_tokens,
        sum_attn[:, :model_width],
        sum_attn[:, model_width : 2 * model_width],
        sum_attn[:, 2 * model_width : 3 * model_width],
        sum_attn[:, 3 * model_width : 4 * model_width],
        sum_attn[:, 4 * model_width :],
        sum_in,
        sum_down,
        grad_b_query,
        grad_b_value,
        grad_b_out,
        grad_b_time,
        grad_b_in,
        grad_b_down,
        sum_gain_one,
        sum_shift_one,
        sum_gain_two,
        sum_shift_two,
    )


def solution(mesh):
    in_specs = (
        P(("dp", "seq"), None),
        P(("dp", "seq"), None),
        P("dp"),
        P(("dp", "seq"), None),
        P("seq", None),
        P("seq", None),
        P("seq", None),
        P("seq", None),
        P("seq", None),
        P("seq", None),
        P("seq", None),
        P(),
        P(),
        P(),
        P(),
        P(),
        P(),
        P(),
        P(),
        P(),
        P(),
    )
    out_specs = (
        P(("dp", "seq"), None),
        P(("dp", "seq"), None),
        P("seq", None),
        P("seq", None),
        P("seq", None),
        P("seq", None),
        P("seq", None),
        P("seq", None),
        P("seq", None),
        P(),
        P(),
        P(),
        P(),
        P(),
        P(),
        P(),
        P(),
        P(),
        P(),
    )
    return jax.shard_map(local, mesh=mesh, in_specs=in_specs, out_specs=out_specs, check_vma=False)
```

profile of v0, /device:TPU:0, one launch (start us, length us, event | category | flops | bytes accessed | tf_op | source)
XLA Modules:
  0.0 1024.9 jit_solution(11175937221474394372)
XLA Ops:
  11.2 23.7 %all-gather.8.cloned.1.call-done = bf16[1024,1024]{1,0:T(8,128)(2,1)} async-done(((bf16[256,1024]{1,0:T(8,128)(2,1)}), bf16[1024,1024]{1,0:T(8,128)(2,1)}) %all-gather.8.cloned.1.call-update) | async-done | bytes 2097168 | tf_op jit(solution)/shard_map/all_gather | solution.py:122
  36.9 22.2 %all-gather.12.cloned.1.call-done = bf16[1024,1024]{1,0:T(8,128)(2,1)} async-done(((bf16[256,1024]{1,0:T(8,128)(2,1)}), bf16[1024,1024]{1,0:T(8,128)(2,1)}) %all-gather.12.cloned.1.call-update) | async-done | bytes 2097168 | tf_op jit(solution)/shard_map/all_gather | solution.py:119
  62.9 20.3 %all-gather.10.cloned.1.call-done = bf16[1024,1024]{1,0:T(8,128)(2,1)} async-done(((bf16[256,1024]{1,0:T(8,128)(2,1)}), bf16[1024,1024]{1,0:T(8,128)(2,1)}) %all-gather.10.cloned.1.call-update) | async-done | bytes 2097168 | tf_op jit(solution)/shard_map/all_gather | solution.py:118
  87.1 20.2 %all-gather.14.cloned.1.call-done = bf16[1024,1024]{1,0:T(8,128)(2,1)} async-done(((bf16[256,1024]{1,0:T(8,128)(2,1)}), bf16[1024,1024]{1,0:T(8,128)(2,1)}) %all-gather.14.cloned.1.call-update) | async-done | bytes 2097168 | tf_op jit(solution)/shard_map/all_gather | solution.py:120
  122.3 77.5 %all-to-all-done = bf16[1,512,3,1024]{1,2,0,3:T(4,128)(2,1)} async-done(((bf16[1,512,3,1024]{1,2,0,3:T(4,128)(2,1)}), bf16[1,512,3,1024]{1,2,0,3:T(4,128)(2,1)}, u32[]{:S(2)}, u32[]{:S(2)}) %all-to-all-start) | async-done | bytes 3145760 | tf_op jit(solution)/shard_map/all_to_all | solution.py:155
  202.9 16.3 %while.22 = (s32[]{:T(128)}, bf16[4,512,256]{1,2,0:T(8,128)(2,1)}, f32[4,4,512]{2,1,0:T(4,128)S(1)}, bf16[4,512,3,256]{1,3,2,0:T(8,128)(2,1)S(1)}, pred[4,512]{1,0:T(4,128)(4,1)S(1)}, /*index=5*/s32[]{:T(128)}) while((s32[]{:T(128)}, bf16[4,512,256]{1,2,0:T(8,128)(2,1)}, f32[4,4,512]{2,1,0:T(4,128)S(1)}, ...), condition=%wide.region_3.4_spmd, body=%wide.region_0.3_spmd.sunk | while | flops 281147392 | bytes 17370192 | solution.py:156
  223.7 18.0 %all-to-all-done.1 = bf16[4,512,256]{1,2,0:T(8,128)(2,1)} async-done(((bf16[4,512,256]{1,2,0:T(8,128)(2,1)}), bf16[4,512,256]{1,2,0:T(8,128)(2,1)}, u32[]{:S(2)}, u32[]{:S(2)}) %all-to-all-start.1) | async-done | bytes 1048608 | tf_op jit(solution)/shard_map/all_to_all | solution.py:157
  247.0 27.2 %multiply_convert_fusion.1 = (bf16[512,4096]{1,0:T(8,128)(2,1)}, f32[512,4096]{1,0:T(8,128)}, f32[512,4096]{1,0:T(8,128)}) fusion(f32[4096]{0:T(1024)S(1)} %convert_element_type.170, bf16[4096,1024]{1,0:T(8,128)(2,1)} %all-gather.18.cloned.1.call-done, f32[512,1024]{1,0:T(8,128)} %copy-done, f32[1024]{0:T(1024)S(1)} %convert_element_type.168, ...), kind=kOutput, calls=%fused_computation.37 | convolution fusion | flops 4436000768 | bytes 31485952 | tf_op jit(solution)/shard_map/td,fd->tf/dot_general | solution.py:164
  274.2 10.3 %all-gather.20.cloned.1.call-done = bf16[4096,1024]{1,0:T(8,128)(2,1)} async-done(((bf16[1024,1024]{1,0:T(8,128)(2,1)}), bf16[4096,1024]{1,0:T(8,128)(2,1)}) %all-gather.20.cloned.1.call-update) | async-done | bytes 8388624 | tf_op jit(solution)/shard_map/all_gather | solution.py:124
  284.5 10.0 fusion.59
  300.6 7.1 convolution_convert_fusion
  307.7 13.5 %convert_reduce_fusion = (f32[4096]{0:T(1024)S(1)}, bf16[512,4096]{1,0:T(8,128)(2,1)S(1)}) fusion(f32[512,4096]{1,0:T(8,128)} %get-tuple-element.209, f32[512,4096]{1,0:T(8,128)} %get-tuple-element.234, f32[4096]{0:T(1024)S(1)} %convert_element_type.170, bf16[512,1024]{1,0:T(8,128)(2,1)S(1)} %get-tuple-element.199, ...), kind=kOutput, calls=%fused_computation.35 | convolution fusion | flops 4330614784 | bytes 30441472 | tf_op jit(solution)/shard_map/td,fd->tf/dot_general | solution.py:183
  321.3 7.0 convolution_convert_fusion.1
  328.3 13.9 %pad_maximum_fusion = bf16[4096,2048]{0,1:T(8,128)(2,1)} fusion(bf16[4096,1024]{0,1:T(8,128)(2,1)} %convolution_convert_fusion, bf16[4096,1024]{0,1:T(8,128)(2,1)} %convolution_convert_fusion.1), kind=kLoop, calls=%fused_computation.31 | loop fusion | flops 33554432 | bytes 33554432 | tf_op jit(solution)/shard_map/concatenate | solution.py:221
  342.2 11.4 %multiply_reduce_fusion.2 = (f32[1024]{0:T(1024)S(1)}, f32[512]{0:T(512)S(1)}, f32[1024]{0:T(1024)S(1)}, f32[512,1024]{1,0:T(8,128)S(1)}) fusion(f32[512,1024]{1,0:T(8,128)} %copy-done, f32[512]{0:T(512)S(1)} %fusion.42, f32[512]{0:T(512)S(1)} %broadcast_multiply_fusion.1, f32[1024]{0:T(1024)S(1)} %convert_element_type.167, ...), kind=kOutput, calls=%fused_computation.61 | convolution fusion | flops 4300207616 | bytes 18894848 | tf_op jit(solution)/shard_map/dot_general | solution.py:185
  365.9 9.0 reduce.7
  383.1 26.1 %all-to-all-done.2 = bf16[4,2,65536]{2,1,0:T(2,128)(2,1)} async-done(((bf16[4,2,65536]{2,1,0:T(2,128)(2,1)}), bf16[4,2,65536]{2,1,0:T(2,128)(2,1)}, u32[]{:S(2)}, u32[]{:S(2)}) %all-to-all-start.2) | async-done | bytes 1048608 | tf_op jit(solution)/shard_map/all_to_all | solution.py:191
  416.1 35.0 %while.23 = (s32[]{:T(128)}, bf16[4,512,3,256]{1,3,2,0:T(8,128)(2,1)}, bf16[4,512,3,256]{1,3,2,0:T(8,128)(2,1)S(1)}, pred[4,512]{1,0:T(4,128)(4,1)S(1)}, f32[4,4...) while((s32[]{:T(128)}, bf16[4,512,3,256]{1,3,2,0:T(8,128)(2,1)}, ...), condition=%wide.region_14.15_spmd, body=%wide.region_12.14_spmd.sunk | while | flops 689829888 | bytes 39382108 | solution.py:198
  459.2 51.5 %all-to-all-done.3 = bf16[4,512,3,256]{1,3,2,0:T(8,128)(2,1)S(1)} async-done(((bf16[4,512,3,256]{1,3,2,0:T(8,128)(2,1)}), bf16[4,512,3,256]{1,3,2,0:T(8,128)(2,1)S(1)}, u32[]{:S(2)}, u32[]{:S(2)}) %all-to-all-start.3) | async-done | bytes 3145760 | tf_op jit(solution)/shard_map/all_to_all | solution.py:199
  524.0 9.9 pad_maximum_fusion.1
  548.6 41.3 %all-reduce = (f32[1024]{0:T(1024)}, f32[1024]{0:T(1024)}, f32[1024]{0:T(1024)}, f32[1024]{0:T(1024)}, f32[4096]{0:T(1024)}, /*index=5*/f32[1024]{0:T(1024)}, f3...) all-reduce(f32[1024]{0:T(1024)S(1)} %get-tuple-element.240, ...), channel_id=1, replica_groups=mesh['dp'=8,'seq'=4] {'dp','seq'}, use_global_device_ids=true, to_apply=%region_22.23 | all-reduce | flops 13312 | bytes 104448 | tf_op jit(solution)/shard_map/psum | solution.py:250
  589.9 29.4 %reduce-scatter.3.cloned.1.call-done = bf16[256,5120]{1,0:T(8,128)(2,1)} async-done(((bf16[1024,5120]{1,0:T(8,128)(2,1)}), bf16[256,5120]{1,0:T(8,128)(2,1)}) %reduce-scatter.3.cloned.1.call-update) | async-done | bytes 2621456 | tf_op jit(solution)/shard_map/reduce_scatter | solution.py:232
  619.3 267.7 %all-reduce.6 = f32[256,5120]{1,0:T(8,128)} all-reduce(bf16[256,5120]{1,0:T(8,128)(2,1)} %reduce-scatter.3.cloned.1.call-done), channel_id=1, replica_groups=mesh['dp'=8,'seq'=4] {'dp'}, use_global_device_ids=true, to_apply=%region_17.18 | all-reduce | flops 1310720 | bytes 7864320 | tf_op jit(solution)/shard_map/psum | solution.py:238
  892.0 114.9 %all-reduce.5.cloned.1.call-done = (f32[1024,1024]{0,1:T(8,128)}, f32[1024,1024]{0,1:T(8,128)}) async-done(((f32[1024,1024]{0,1:T(8,128)}, f32[1024,1024]{0,1:T(8,128)}), (f32[1024,1024]{0,1:T(8,128)}, f32[1024,1024]{0,1:T(8,128)})) %all-reduce.5.cloned.1.call-update) | async-done | bytes 8388624 | tf_op jit(solution)/shard_map/psum | solution.py:238
  (250 shorter events, 177.1 us)
Async XLA Ops:
  7.2 27.7 %copy-start.22 = (bf16[1,1024]{1,0:T(2,128)(2,1)S(1)}, bf16[1,1024]{1,0:T(2,128)(2,1)}, u32[]{:S(2)}) copy-start(bf16[1,1024]{1,0:T(2,128)(2,1)} %param.26) | copy-start | bytes 6148
  7.2 29.7 %copy-start.27 = (bf16[1024]{0:T(1024)(128)(2,1)S(1)}, bf16[1024]{0:T(1024)(128)(2,1)}, u32[]{:S(2)}) copy-start(bf16[1024]{0:T(1024)(128)(2,1)} %param.39) | copy-start | bytes 6148
  7.2 51.9 %copy-start.12 = (bf16[512,1024]{1,0:T(8,128)(2,1)S(1)}, bf16[512,1024]{1,0:T(8,128)(2,1)}, u32[]{:S(2)}) copy-start(bf16[512,1024]{1,0:T(8,128)(2,1)} %param.25) | copy-start | bytes 3145732
  7.2 27.7 %all-gather.8.cloned.1.call-start = ((), (), s32[]{:S(2)}) async-start(), calls=%async_computation.6 | async-start | bytes 2621440 | tf_op jit(solution)/shard_map/all_gather | solution.py:122
  8.0 51.1 %all-gather.12.cloned.1.call-start = ((), (), s32[]{:S(2)}) async-start(), calls=%async_computation.8 | async-start | bytes 2621440 | tf_op jit(solution)/shard_map/all_gather | solution.py:119
  8.7 74.5 %all-gather.10.cloned.1.call-start = ((), (), s32[]{:S(2)}) async-start(), calls=%async_computation.7 | async-start | bytes 2621440 | tf_op jit(solution)/shard_map/all_gather | solution.py:118
  9.5 97.8 %all-gather.14.cloned.1.call-start = ((), (), s32[]{:S(2)}) async-start(), calls=%async_computation.9 | async-start | bytes 2621440 | tf_op jit(solution)/shard_map/all_gather | solution.py:120
  10.0 213.6 %all-gather.16.cloned.1.call-start = ((), (), s32[]{:S(2)}) async-start(), calls=%async_computation.10 | async-start | bytes 2621440 | tf_op jit(solution)/shard_map/all_gather | solution.py:121
  10.6 236.4 %all-gather.18.cloned.1.call-start = ((), (), s32[]{:S(2)}) async-start(), calls=%async_computation.11 | async-start | bytes 10485760 | tf_op jit(solution)/shard_map/all_gather | solution.py:123
  36.9 204.8 %copy-start.16 = (f32[1024]{0:T(1024)}, f32[1024]{0:T(1024)S(1)}, u32[]{:S(2)}) copy-start(f32[1024]{0:T(1024)S(1)} %convert_add_fusion.1) | copy-start | bytes 12292
  116.3 83.5 %all-to-all-start = ((bf16[1,512,3,1024]{1,2,0,3:T(4,128)(2,1)}), bf16[1,512,3,1024]{1,2,0,3:T(4,128)(2,1)}, u32[]{:S(2)}, u32[]{:S(2)}) async-start(bf16[1,512,3,1024]{1,2,0,3:T(4,128)(2,1)} %copy.80), calls=%async_computation | async-start | bytes 8388608 | tf_op jit(solution)/shard_map/all_to_all | solution.py:155
  121.4 163.1 %all-gather.20.cloned.1.call-start = ((), (), s32[]{:S(2)}) async-start(), calls=%async_computation.12 | async-start | bytes 10485760 | tf_op jit(solution)/shard_map/all_gather | solution.py:124
  202.8 20.7 %copy-start.29 = (bf16[1024]{0:T(1024)(128)(2,1)S(1)}, bf16[1024]{0:T(1024)(128)(2,1)}, u32[]{:S(2)}) copy-start(bf16[1024]{0:T(1024)(128)(2,1)} %param.42) | copy-start | bytes 6148
  202.8 20.7 %copy-start.30 = (bf16[1024]{0:T(1024)(128)(2,1)S(1)}, bf16[1024]{0:T(1024)(128)(2,1)}, u32[]{:S(2)}) copy-start(bf16[1024]{0:T(1024)(128)(2,1)} %param.43) | copy-start | bytes 6148
  202.8 20.7 %copy-start.24 = (bf16[4096]{0:T(1024)(128)(2,1)S(1)}, bf16[4096]{0:T(1024)(128)(2,1)}, u32[]{:S(2)}) copy-start(bf16[4096]{0:T(1024)(128)(2,1)} %param.40) | copy-start | bytes 24580
  202.8 20.7 %copy-start.31 = (bf16[1024]{0:T(1024)(128)(2,1)S(1)}, bf16[1024]{0:T(1024)(128)(2,1)}, u32[]{:S(2)}) copy-start(bf16[1024]{0:T(1024)(128)(2,1)} %param.41) | copy-start | bytes 6148
  202.9 20.7 %copy-start.32 = (bf16[1024]{0:T(1024)(128)(2,1)S(1)}, bf16[1024]{0:T(1024)(128)(2,1)}, u32[]{:S(2)}) copy-start(bf16[1024]{0:T(1024)(128)(2,1)} %param.44) | copy-start | bytes 6148
  202.9 20.7 %copy-start.33 = (bf16[1024]{0:T(1024)(128)(2,1)S(1)}, bf16[1024]{0:T(1024)(128)(2,1)}, u32[]{:S(2)}) copy-start(bf16[1024]{0:T(1024)(128)(2,1)} %param.45) | copy-start | bytes 6148
  219.2 22.5 %all-to-all-start.1 = ((bf16[4,512,256]{1,2,0:T(8,128)(2,1)}), bf16[4,512,256]{1,2,0:T(8,128)(2,1)}, u32[]{:S(2)}, u32[]{:S(2)}) async-start(bf16[4,512,256]{1,2,0:T(8,128)(2,1)} %get-tuple-element.79), calls=%async_computation.1 | async-start | bytes 2097152 | tf_op jit(solution)/shard_map/all_to_all | solution.py:157
  223.4 310.5 %reduce-scatter.5.cloned.1.call-start = ((), (), s32[]{:S(2)}) async-start(), calls=%async_computation.14 | async-start | bytes 20971520 | tf_op jit(solution)/shard_map/reduce_scatter | solution.py:220
  378.8 30.4 %all-to-all-start.2 = ((bf16[4,2,65536]{2,1,0:T(2,128)(2,1)}), bf16[4,2,65536]{2,1,0:T(2,128)(2,1)}, u32[]{:S(2)}, u32[]{:S(2)}) async-start(bf16[4,2,65536]{2,1,0:T(2,128)(2,1)} %reshape.269), calls=%async_computation.2 | async-start | bytes 2097152 | tf_op jit(solution)/shard_map/all_to_all | solution.py:191
  451.1 59.6 %all-to-all-start.3 = ((bf16[4,512,3,256]{1,3,2,0:T(8,128)(2,1)}), bf16[4,512,3,256]{1,3,2,0:T(8,128)(2,1)S(1)}, u32[]{:S(2)}, u32[]{:S(2)}) async-start(bf16[4,512,3,256]{1,3,2,0:T(8,128)(2,1)} %get-tuple-element.81), calls=%async_computation.3 | async-start | bytes 6291456 | tf_op jit(solution)/shard_map/all_to_all | solution.py:199
  454.9 164.4 %reduce-scatter.3.cloned.1.call-start = ((), (), s32[]{:S(2)}) async-start(), calls=%async_computation.13 | async-start | bytes 13107200 | tf_op jit(solution)/shard_map/reduce_scatter | solution.py:232
  533.9 473.0 %all-reduce.5.cloned.1.call-start = ((), (), s32[]{:S(2)}) async-start(), calls=%async_computation.15 | async-start | bytes 16777216 | tf_op jit(solution)/shard_map/psum | solution.py:238
  (30 other events, 144.6 us)
Sparse Core Ops, SparseCore 0:
  9.6 25.2 all-gather.7
  36.5 22.5 all-gather.11
  60.7 22.5 all-gather.9
  84.7 22.5 all-gather.13
  108.7 27.7 all-gather.15
  137.9 83.4 all-gather.17
  223.0 61.5 all-gather.19
  342.3 155.0 reduce-scatter.4
  534.0 85.2 reduce-scatter.2
  624.4 382.4 all-reduce.4
where the time goes:
time: 1030 us; the launch traced here: 1020 us
  waiting for transfers between devices  419 us (41%)
  blocking collectives  309 us (30%)
  matrix products  135 us (13%)
  local copies, waits for them, and re-layouts  75.6 us (7%)
  other arithmetic  52.9 us (5%)
  starting transfers between devices  17.8 us (2%)
  between operations  15.3 us (1%)
    psum x1, blocking collectives, local(): lax.psum((share_in, share_down, attn_share), 'dp')  268 us
    psum x1, waiting for transfers between devices, local(): lax.psum((share_in, share_down, attn_share), 'dp')  115 us
    all_to_all x1, waiting for transfers between devices, local(): lax.all_to_all(stacked, 'seq', split_axis=3, concat_axis=0, tiled=True)  77.5 us
    all_to_all x1, waiting for transfers between devices, local(): lax.all_to_all(grad_stack, 'seq', split_axis=0, concat_axis=3, tiled=True)  51.5 us
    psum x1, blocking collectives, local(): lax.psum((jnp.sum(grad_query_rows, axis=0, dtype=jnp.float32), jnp.sum(gr...  41.3 us
    unnamed x86, local copies, waits for them, and re-layouts  32.8 us
    reduce_scatter x1, waiting for transfers between devices, local(): lax.psum_scatter(jnp.concatenate([term_qkv, term_out, term_time], axis=1)...  29.4 us
    dot_general x1, matrix products, local(): jnp.einsum('td,fd->tf', first_low, full_in, preferred_element_type=jnp.fl...  27.2 us
  transfers between devices with their start and end apart: 14, of which 11 were waited for; matrix products, arithmetic and copies ran while one was open for 18% of the time, Pallas kernels for 0%

commit v1 on v0

--- a/solution.py
+++ b/solution.py
@@ -152,7 +152,32 @@
     stacked = jnp.stack([query_rows, key_rows, value_rows], axis=1).reshape(
         item_count, slot_count, 3, model_width
     )
-    head_side = lax.all_to_all(stacked, "seq", split_axis=3, concat_axis=0, tiled=True)
+
+    def lift_sums_all_for(block_here):
+        next_value = lax.axis_size("seq")
+        m_next = lax.axis_index("seq")
+        arr_next, frame_out = (next_value, m_next)
+        met_up = block_here.shape[3] // arr_next
+        z1 = list(block_here.shape)
+        z1[3] = met_up
+        finding = z1[0]
+        z1[0] = finding * arr_next
+        current_block = jnp.zeros(z1, block_here.dtype)
+        for tick in [*range(arr_next)]:
+            tile_out = lax.dynamic_slice_in_dim(
+                block_here, (frame_out ^ tick) * met_up, met_up, axis=3
+            )
+            if tick:
+                crops = []
+                for dev_j in tuple(range(arr_next)):
+                    crops.append((dev_j, dev_j ^ tick))
+                tile_out = lax.ppermute(tile_out, "seq", crops)
+            current_block = lax.dynamic_update_slice_in_dim(
+                current_block, tile_out, (frame_out ^ tick) * finding, axis=0
+            )
+        return current_block
+
+    head_side = lift_sums_all_for(stacked)
     mixed_heads, log_totals = lax.map(attend_forward, (head_side, group_valid))
     mixed_rows = lax.all_to_all(
         mixed_heads, "seq", split_axis=0, concat_axis=2, tiled=True

time: 1030 us -> 1030 us (level)
  waiting for transfers between devices: 419 us -> 385 us
  blocking collectives: 309 us -> 337 us
    all_to_all x2 -> x0, waiting for transfers between devices: 104 us -> none  [the longest x1 77.5 us: local(): lax.all_to_all(stacked, 'seq', split_axis=3, concat_axis=0, tiled=True)]
    ppermute x0 -> x3, waiting for transfers between devices: none -> 40.1 us  [lift_sums_all_for(): tile_out = lax.ppermute(tile_out, 'seq', crops)]
    all_to_all x0 -> x1, blocking collectives: none -> 30.4 us  [local(): lax.all_to_all(grad_mixed.reshape(item_count, slot_count, model_width), '...]
    all_gather x1, waiting for transfers between devices: 10.3 us -> 31.6 us  [local(): lax.all_gather(w_down, 'seq', axis=0, tiled=True)]
    unnamed x86 -> x84, local copies, waits for them, and re-layouts: 32.8 us -> 34.3 us
  transfers between devices with their start and end apart: 14 -> 15, of which waited for: 11 -> 11; matrix products, arithmetic and copies ran while one was open for 18% -> 19% of each run, Pallas kernels for 0% -> 0%
where the time goes in v1:
time: 1030 us; the launch traced here: 1020 us
  waiting for transfers between devices  385 us (37%)
  blocking collectives  337 us (33%)
  matrix products  133 us (13%)
  local copies, waits for them, and re-layouts  83.8 us (8%)
  other arithmetic  52.9 us (5%)
  between operations  15.4 us (1%)
  starting transfers between devices  10.5 us (1%)
    psum x1, blocking collectives, local(): lax.psum((share_in, share_down, attn_share), 'dp')  265 us
    psum x1, waiting for transfers between devices, local(): lax.psum((share_in, share_down, attn_share), 'dp')  117 us
    all_to_all x1, waiting for transfers between devices, local(): lax.all_to_all(grad_stack, 'seq', split_axis=0, concat_axis=3, tiled=True)  49 us
    psum x1, blocking collectives, local(): lax.psum((jnp.sum(grad_query_rows, axis=0, dtype=jnp.float32), jnp.sum(gr...  41.6 us
    ppermute x3, waiting for transfers between devices, lift_sums_all_for(): tile_out = lax.ppermute(tile_out, 'seq', crops)  40.1 us
    unnamed x84, local copies, waits for them, and re-layouts  34.3 us
    all_gather x1, waiting for transfers between devices, local(): lax.all_gather(w_down, 'seq', axis=0, tiled=True)  31.6 us
    all_to_all x1, blocking collectives, local(): lax.all_to_all(grad_mixed.reshape(item_count, slot_count, model_width), '...  30.4 us
  transfers between devices with their start and end apart: 15, of which 11 were waited for; matrix products, arithmetic and copies ran while one was open for 19% of the time, Pallas kernels for 0%

profile of v1, /device:TPU:0, one launch (start us, length us, event | category | flops | bytes accessed | tf_op | source)
XLA Modules:
  0.0 1017.8 jit_solution(15716176928645232391)
XLA Ops:
  11.3 23.6 %all-gather.8.cloned.1.call-done = bf16[1024,1024]{1,0:T(8,128)(2,1)} async-done(((bf16[256,1024]{1,0:T(8,128)(2,1)}), bf16[1024,1024]{1,0:T(8,128)(2,1)}) %all-gather.8.cloned.1.call-update) | async-done | bytes 2097168 | tf_op jit(solution)/shard_map/all_gather | solution.py:122
  36.9 22.2 %all-gather.12.cloned.1.call-done = bf16[1024,1024]{1,0:T(8,128)(2,1)} async-done(((bf16[256,1024]{1,0:T(8,128)(2,1)}), bf16[1024,1024]{1,0:T(8,128)(2,1)}) %all-gather.12.cloned.1.call-update) | async-done | bytes 2097168 | tf_op jit(solution)/shard_map/all_gather | solution.py:119
  61.9 21.3 %all-gather.10.cloned.1.call-done = bf16[1024,1024]{1,0:T(8,128)(2,1)} async-done(((bf16[256,1024]{1,0:T(8,128)(2,1)}), bf16[1024,1024]{1,0:T(8,128)(2,1)}) %all-gather.10.cloned.1.call-update) | async-done | bytes 2097168 | tf_op jit(solution)/shard_map/all_gather | solution.py:118
  86.1 21.2 %all-gather.14.cloned.1.call-done = bf16[1024,1024]{1,0:T(8,128)(2,1)} async-done(((bf16[256,1024]{1,0:T(8,128)(2,1)}), bf16[1024,1024]{1,0:T(8,128)(2,1)}) %all-gather.14.cloned.1.call-update) | async-done | bytes 2097168 | tf_op jit(solution)/shard_map/all_gather | solution.py:120
  118.8 25.4 %collective-permute-done.1 = bf16[1,512,3,256]{3,1,2,0:T(8,128)(2,1)} collective-permute-done((bf16[1,512,3,256]{3,1,2,0:T(8,128)(2,1)}, bf16[1,512,3,256]{3,1,2,0:T(8,128)(2,1)}, u32[]{:S(2)}, u32[]{:S(2)}) %collective-permute-start.1) | collective-permute-done | bytes 786464 | tf_op jit(solution)/shard_map/ppermute | solution.py:174
  148.9 14.7 %collective-permute-done.2 = bf16[1,512,3,256]{3,1,2,0:T(8,128)(2,1)} collective-permute-done((bf16[1,512,3,256]{3,1,2,0:T(8,128)(2,1)}, bf16[1,512,3,256]{3,1,2,0:T(8,128)(2,1)}, u32[]{:S(2)}, u32[]{:S(2)}) %collective-permute-start.2) | collective-permute-done | bytes 786464 | tf_op jit(solution)/shard_map/ppermute | solution.py:174
  167.2 16.3 %while.22 = (s32[]{:T(128)}, bf16[4,512,256]{1,2,0:T(8,128)(2,1)}, f32[4,4,512]{2,1,0:T(4,128)S(1)}, bf16[4,512,3,256]{1,3,2,0:T(8,128)(2,1)S(1)}, pred[4,512]{1,0:T(4,128)(4,1)S(1)}, /*index=5*/s32[]{:T(128)}) while((s32[]{:T(128)}, bf16[4,512,256]{1,2,0:T(8,128)(2,1)}, f32[4,4,512]{2,1,0:T(4,128)S(1)}, ...), condition=%wide.region_3.4_spmd, body=%wide.region_0.3_spmd.sunk | while | flops 281147392 | bytes 17370192 | solution.py:181
  188.0 26.0 %all-to-all-done = bf16[4,512,256]{1,2,0:T(8,128)(2,1)} async-done(((bf16[4,512,256]{1,2,0:T(8,128)(2,1)}), bf16[4,512,256]{1,2,0:T(8,128)(2,1)}, u32[]{:S(2)}, u32[]{:S(2)}) %all-to-all-start) | async-done | bytes 1048608 | tf_op jit(solution)/shard_map/all_to_all | solution.py:182
  219.3 27.2 %multiply_convert_fusion.1 = (bf16[512,4096]{1,0:T(8,128)(2,1)}, f32[512,4096]{1,0:T(8,128)}, f32[512,4096]{1,0:T(8,128)}) fusion(f32[4096]{0:T(1024)S(1)} %convert_element_type.170, bf16[4096,1024]{1,0:T(8,128)(2,1)} %all-gather.18.cloned.1.call-done, f32[512,1024]{1,0:T(8,128)} %copy-done, f32[1024]{0:T(1024)S(1)} %convert_element_type.168, ...), kind=kOutput, calls=%fused_computation.37 | convolution fusion | flops 4436000768 | bytes 31485952 | tf_op jit(solution)/shard_map/td,fd->tf/dot_general | solution.py:189
  246.5 31.6 %all-gather.20.cloned.1.call-done = bf16[4096,1024]{1,0:T(8,128)(2,1)} async-done(((bf16[1024,1024]{1,0:T(8,128)(2,1)}), bf16[4096,1024]{1,0:T(8,128)(2,1)}) %all-gather.20.cloned.1.call-update) | async-done | bytes 8388624 | tf_op jit(solution)/shard_map/all_gather | solution.py:124
  278.1 10.0 fusion.59
  294.1 7.1 convolution_convert_fusion
  301.3 13.5 %convert_reduce_fusion = (f32[4096]{0:T(1024)S(1)}, bf16[512,4096]{1,0:T(8,128)(2,1)S(1)}) fusion(f32[512,4096]{1,0:T(8,128)} %get-tuple-element.209, f32[512,4096]{1,0:T(8,128)} %get-tuple-element.238, f32[4096]{0:T(1024)S(1)} %convert_element_type.170, bf16[512,1024]{1,0:T(8,128)(2,1)S(1)} %get-tuple-element.199, ...), kind=kOutput, calls=%fused_computation.35 | convolution fusion | flops 4330614784 | bytes 30441472 | tf_op jit(solution)/shard_map/td,fd->tf/dot_general | solution.py:208
  321.8 13.8 %pad_maximum_fusion = bf16[4096,2048]{0,1:T(8,128)(2,1)} fusion(bf16[4096,1024]{0,1:T(8,128)(2,1)} %convolution_convert_fusion, bf16[4096,1024]{0,1:T(8,128)(2,1)} %convolution_convert_fusion.1), kind=kLoop, calls=%fused_computation.31 | loop fusion | flops 33554432 | bytes 33554432 | tf_op jit(solution)/shard_map/concatenate | solution.py:246
  335.7 11.4 %multiply_reduce_fusion.2 = (f32[1024]{0:T(1024)S(1)}, f32[512]{0:T(512)S(1)}, f32[1024]{0:T(1024)S(1)}, f32[512,1024]{1,0:T(8,128)S(1)}) fusion(f32[512,1024]{1,0:T(8,128)} %copy-done, f32[512]{0:T(512)S(1)} %fusion.42, f32[512]{0:T(512)S(1)} %broadcast_multiply_fusion.1, f32[1024]{0:T(1024)S(1)} %convert_element_type.167, ...), kind=kOutput, calls=%fused_computation.60 | convolution fusion | flops 4300207616 | bytes 18894848 | tf_op jit(solution)/shard_map/dot_general | solution.py:210
  359.9 9.0 reduce.7
  372.9 30.4 %all_to_all.48 = bf16[4,2,65536]{2,1,0:T(2,128)(2,1)} all-to-all(bf16[4,2,65536]{2,1,0:T(2,128)(2,1)} %reshape.270), channel_id=1, replica_groups=mesh['dp'=8,'seq'=4] {'seq'}, dimensions={0} | all-to-all | bytes 2097152 | tf_op jit(solution)/shard_map/all_to_all | solution.py:216
  412.0 35.0 %while.23 = (s32[]{:T(128)}, bf16[4,512,3,256]{1,3,2,0:T(8,128)(2,1)}, bf16[4,512,3,256]{1,3,2,0:T(8,128)(2,1)S(1)}, pred[4,512]{1,0:T(4,128)(4,1)S(1)}, f32[4,4...) while((s32[]{:T(128)}, bf16[4,512,3,256]{1,3,2,0:T(8,128)(2,1)}, ...), condition=%wide.region_14.15_spmd, body=%wide.region_12.14_spmd.sunk | while | flops 689829888 | bytes 39382108 | solution.py:223
  455.2 49.0 %all-to-all-done.2 = bf16[4,512,3,256]{1,3,2,0:T(8,128)(2,1)S(1)} async-done(((bf16[4,512,3,256]{1,3,2,0:T(8,128)(2,1)}), bf16[4,512,3,256]{1,3,2,0:T(8,128)(2,1)S(1)}, u32[]{:S(2)}, u32[]{:S(2)}) %all-to-all-start.2) | async-done | bytes 3145760 | tf_op jit(solution)/shard_map/all_to_all | solution.py:224
  517.2 9.9 pad_maximum_fusion.1
  541.8 41.6 %all-reduce = (f32[1024]{0:T(1024)}, f32[1024]{0:T(1024)}, f32[1024]{0:T(1024)}, f32[1024]{0:T(1024)}, f32[4096]{0:T(1024)}, /*index=5*/f32[1024]{0:T(1024)}, f3...) all-reduce(f32[1024]{0:T(1024)S(1)} %get-tuple-element.244, ...), channel_id=1, replica_groups=mesh['dp'=8,'seq'=4] {'dp','seq'}, use_global_device_ids=true, to_apply=%region_22.23 | all-reduce | flops 13312 | bytes 104448 | tf_op jit(solution)/shard_map/psum | solution.py:275
  583.4 29.1 %reduce-scatter.3.cloned.1.call-done = bf16[256,5120]{1,0:T(8,128)(2,1)} async-done(((bf16[1024,5120]{1,0:T(8,128)(2,1)}), bf16[256,5120]{1,0:T(8,128)(2,1)}) %reduce-scatter.3.cloned.1.call-update) | async-done | bytes 2621456 | tf_op jit(solution)/shard_map/reduce_scatter | solution.py:257
  612.5 264.9 %all-reduce.6 = f32[256,5120]{1,0:T(8,128)} all-reduce(bf16[256,5120]{1,0:T(8,128)(2,1)} %reduce-scatter.3.cloned.1.call-done), channel_id=1, replica_groups=mesh['dp'=8,'seq'=4] {'dp'}, use_global_device_ids=true, to_apply=%region_17.18 | all-reduce | flops 1310720 | bytes 7864320 | tf_op jit(solution)/shard_map/psum | solution.py:263
  882.4 117.5 %all-reduce.5.cloned.1.call-done = (f32[1024,1024]{0,1:T(8,128)}, f32[1024,1024]{0,1:T(8,128)}) async-done(((f32[1024,1024]{0,1:T(8,128)}, f32[1024,1024]{0,1:T(8,128)}), (f32[1024,1024]{0,1:T(8,128)}, f32[1024,1024]{0,1:T(8,128)})) %all-reduce.5.cloned.1.call-update) | async-done | bytes 8388624 | tf_op jit(solution)/shard_map/psum | solution.py:263
  (259 shorter events, 181.9 us)
Async XLA Ops:
  7.2 27.7 %copy-start.21 = (bf16[1,1024]{1,0:T(2,128)(2,1)S(1)}, bf16[1,1024]{1,0:T(2,128)(2,1)}, u32[]{:S(2)}) copy-start(bf16[1,1024]{1,0:T(2,128)(2,1)} %param.26) | copy-start | bytes 6148
  7.2 27.7 %all-gather.8.cloned.1.call-start = ((), (), s32[]{:S(2)}) async-start(), calls=%async_computation.5 | async-start | bytes 2621440 | tf_op jit(solution)/shard_map/all_gather | solution.py:122
  8.0 28.9 %copy-start.26 = (bf16[1024]{0:T(1024)(128)(2,1)S(1)}, bf16[1024]{0:T(1024)(128)(2,1)}, u32[]{:S(2)}) copy-start(bf16[1024]{0:T(1024)(128)(2,1)} %param.39) | copy-start | bytes 6148
  8.0 51.1 %copy-start.13 = (bf16[512,1024]{1,0:T(8,128)(2,1)S(1)}, bf16[512,1024]{1,0:T(8,128)(2,1)}, u32[]{:S(2)}) copy-start(bf16[512,1024]{1,0:T(8,128)(2,1)} %param.25) | copy-start | bytes 3145732
  8.0 51.1 %all-gather.12.cloned.1.call-start = ((), (), s32[]{:S(2)}) async-start(), calls=%async_computation.7 | async-start | bytes 2621440 | tf_op jit(solution)/shard_map/all_gather | solution.py:119
  8.7 74.5 %all-gather.10.cloned.1.call-start = ((), (), s32[]{:S(2)}) async-start(), calls=%async_computation.6 | async-start | bytes 2621440 | tf_op jit(solution)/shard_map/all_gather | solution.py:118
  9.5 97.8 %all-gather.14.cloned.1.call-start = ((), (), s32[]{:S(2)}) async-start(), calls=%async_computation.8 | async-start | bytes 2621440 | tf_op jit(solution)/shard_map/all_gather | solution.py:120
  10.0 178.0 %all-gather.16.cloned.1.call-start = ((), (), s32[]{:S(2)}) async-start(), calls=%async_computation.9 | async-start | bytes 2621440 | tf_op jit(solution)/shard_map/all_gather | solution.py:121
  10.6 208.7 %all-gather.18.cloned.1.call-start = ((), (), s32[]{:S(2)}) async-start(), calls=%async_computation.10 | async-start | bytes 10485760 | tf_op jit(solution)/shard_map/all_gather | solution.py:123
  11.2 266.9 %all-gather.20.cloned.1.call-start = ((), (), s32[]{:S(2)}) async-start(), calls=%async_computation.11 | async-start | bytes 10485760 | tf_op jit(solution)/shard_map/all_gather | solution.py:124
  36.9 177.2 %copy-start.15 = (f32[1024]{0:T(1024)}, f32[1024]{0:T(1024)S(1)}, u32[]{:S(2)}) copy-start(f32[1024]{0:T(1024)S(1)} %convert_add_fusion.1) | copy-start | bytes 12292
  112.0 4.5 collective-permute-start
  112.2 32.0 %collective-permute-start.1 = (bf16[1,512,3,256]{3,1,2,0:T(8,128)(2,1)}, bf16[1,512,3,256]{3,1,2,0:T(8,128)(2,1)}, u32[]{:S(2)}, u32[]{:S(2)}) collective-permute-start(bf16[1,512,3,256]{3,1,2,0:T(8,128)(2,1)} %get-tuple-element.230), channel_id=1, source_target_pairs={{0,2},{1,3},{2,0},{3,1},{4,6},{5,7},{6,4},{7,5},{8,10},{9,11},{10,... | collective-permute-start | bytes 2359304 | tf_op jit(solution)/shard_map/ppermute | solution.py:174
  112.7 51.0 %collective-permute-start.2 = (bf16[1,512,3,256]{3,1,2,0:T(8,128)(2,1)}, bf16[1,512,3,256]{3,1,2,0:T(8,128)(2,1)}, u32[]{:S(2)}, u32[]{:S(2)}) collective-permute-start(bf16[1,512,3,256]{3,1,2,0:T(8,128)(2,1)} %get-tuple-element.229), channel_id=1, source_target_pairs={{0,3},{1,2},{2,1},{3,0},{4,7},{5,6},{6,5},{7,4},{8,11},{9,10},{10,... | collective-permute-start | bytes 2359304 | tf_op jit(solution)/shard_map/ppermute | solution.py:174
  167.2 20.7 %copy-start.29 = (bf16[1024]{0:T(1024)(128)(2,1)S(1)}, bf16[1024]{0:T(1024)(128)(2,1)}, u32[]{:S(2)}) copy-start(bf16[1024]{0:T(1024)(128)(2,1)} %param.43) | copy-start | bytes 6148
  167.2 20.7 %copy-start.23 = (bf16[4096]{0:T(1024)(128)(2,1)S(1)}, bf16[4096]{0:T(1024)(128)(2,1)}, u32[]{:S(2)}) copy-start(bf16[4096]{0:T(1024)(128)(2,1)} %param.40) | copy-start | bytes 24580
  167.2 20.7 %copy-start.30 = (bf16[1024]{0:T(1024)(128)(2,1)S(1)}, bf16[1024]{0:T(1024)(128)(2,1)}, u32[]{:S(2)}) copy-start(bf16[1024]{0:T(1024)(128)(2,1)} %param.41) | copy-start | bytes 6148
  167.2 20.7 %copy-start.31 = (bf16[1024]{0:T(1024)(128)(2,1)S(1)}, bf16[1024]{0:T(1024)(128)(2,1)}, u32[]{:S(2)}) copy-start(bf16[1024]{0:T(1024)(128)(2,1)} %param.44) | copy-start | bytes 6148
  167.2 20.7 %copy-start.32 = (bf16[1024]{0:T(1024)(128)(2,1)S(1)}, bf16[1024]{0:T(1024)(128)(2,1)}, u32[]{:S(2)}) copy-start(bf16[1024]{0:T(1024)(128)(2,1)} %param.45) | copy-start | bytes 6148
  183.5 30.6 %all-to-all-start = ((bf16[4,512,256]{1,2,0:T(8,128)(2,1)}), bf16[4,512,256]{1,2,0:T(8,128)(2,1)}, u32[]{:S(2)}, u32[]{:S(2)}) async-start(bf16[4,512,256]{1,2,0:T(8,128)(2,1)} %get-tuple-element.79), calls=%async_computation | async-start | bytes 2097152 | tf_op jit(solution)/shard_map/all_to_all | solution.py:182
  187.8 339.4 %reduce-scatter.5.cloned.1.call-start = ((), (), s32[]{:S(2)}) async-start(), calls=%async_computation.13 | async-start | bytes 20971520 | tf_op jit(solution)/shard_map/reduce_scatter | solution.py:245
  447.0 57.1 %all-to-all-start.2 = ((bf16[4,512,3,256]{1,3,2,0:T(8,128)(2,1)}), bf16[4,512,3,256]{1,3,2,0:T(8,128)(2,1)S(1)}, u32[]{:S(2)}, u32[]{:S(2)}) async-start(bf16[4,512,3,256]{1,3,2,0:T(8,128)(2,1)} %get-tuple-element.81), calls=%async_computation.2 | async-start | bytes 6291456 | tf_op jit(solution)/shard_map/all_to_all | solution.py:224
  450.9 161.6 %reduce-scatter.3.cloned.1.call-start = ((), (), s32[]{:S(2)}) async-start(), calls=%async_computation.12 | async-start | bytes 13107200 | tf_op jit(solution)/shard_map/reduce_scatter | solution.py:257
  527.1 472.8 %all-reduce.5.cloned.1.call-start = ((), (), s32[]{:S(2)}) async-start(), calls=%async_computation.14 | async-start | bytes 16777216 | tf_op jit(solution)/shard_map/psum | solution.py:263
  (30 other events, 158.0 us)
Sparse Core Ops, SparseCore 0:
  9.6 25.2 all-gather.7
  36.5 22.5 all-gather.11
  60.6 22.5 all-gather.9
  84.6 22.5 all-gather.13
  108.6 33.8 all-gather.15
  144.0 74.2 all-gather.17
  219.8 58.2 all-gather.19
  335.8 152.4 reduce-scatter.4
  527.2 85.2 reduce-scatter.2
  617.6 382.2 all-reduce.4
